TPU v7x, 512 devices: a whole 4x4x16 slice. The times are simulated.
512 devices in a mesh: section: 32 (over z, core), tensor: 16 (over x, y).
Axes of the slice: x: 4, y: 4, z: 16, core: 2. Of those that a mesh axis runs over, the one named last changes fastest.
Arguments:
- activations: bfloat16 [32, 512, 4096], P('section', None, 'tensor'), may hold values from -48 to 48
- gain: bfloat16 [32, 4096], P('section', 'tensor'), may hold values from 0.5 to 1.5
- w_query: bfloat16 [32, 4096, 4096], P('section', None, 'tensor'), may hold values from -0.0625 to 0.0625
- w_kv: bfloat16 [32, 1024, 4096], P('section', 'tensor'), may hold values from -1.8782524 to 1.8782524
- segments: int32 [32, 512], replicated, may hold values from 0 to 31, never falling along the last dimension, each value on 1 to 128 neighbouring positions
- pool: bfloat16 [64, 128, 4096], P('section', None, 'tensor'), may hold values from -48 to 48
- row_ids: int32 [32], replicated, may hold values from 0 to 63, as said below
- row_lengths: int32 [32], replicated, may hold values from 1 to 128, 512 in all
Outputs:
- after_first: bfloat16 [32, 512, 4096], P('section', None, 'tensor')
- after_second: bfloat16 [32, 512, 4096], P('section', None, 'tensor')
Inputs may be any that keep to these rules, and one draw needn't show every extreme that they name: `row_ids`: every block of 2 consecutive ids, the rows of one buffer host, is named at least once; ids may repeat.
All inputs are finite; a program needn't handle non-finite values.
Results may differ from a plain program's by a relative error of at most 0.01.
Values may be sent and summed in bfloat16 or wider, within the bound.
No kernel may reach another device: no remote copies, remote signals or barrier semaphores. Data moves between devices by JAX's collectives and lax.ppermute only.
A program may use at most 64 MiB of HBM per device.

v0:
```python
import jax
import jax.numpy as jnp
from jax import lax
from jax.sharding import PartitionSpec as P

D = 4096
HEADS = 32
KV_HEADS = 4
HEAD_DIM = 128
norm_eps = 1e-05
masked_score = -1e30


def partner_2(block, axis, distance):
    count = lax.axis_size(axis)
    route = []
    for low in range(count):
        high = low | 1 << distance
        if high != low and high < count:
            route += [(low, high), (high, low)]
    return lax.ppermute(block, axis, route)


def from_behind(block, axis, distance):
    devices = range(lax.axis_size(axis))
    route = [(i - distance, i) for i in devices if i - distance in devices]
    return lax.ppermute(block, axis, route)


def attend(inputs, gain_cols, query_weight, keyval_weight, seg_ids, tensor_index):
    row_count, col_count = inputs.shape
    wide_inputs = inputs.astype(jnp.float32)
    square_total = lax.psum(jnp.sum(wide_inputs * wide_inputs, axis=1), "tensor")
    row_scale = lax.rsqrt(square_total / D + norm_eps)
    normed = (wide_inputs * row_scale[:, None] * gain_cols.astype(jnp.float32)[None, :]).astype(
        jnp.bfloat16
    )
    part_cols = lax.all_gather(normed, "tensor", axis=1, tiled=True)
    query_part = jnp.dot(part_cols, query_weight, preferred_element_type=jnp.float32)
    keyval_part = lax.dot_general(
        keyval_weight, part_cols, (((1,), (1,)), ((), ())), preferred_element_type=jnp.float32
    )
    query = query_part.astype(jnp.bfloat16)
    keyval = keyval_part.astype(jnp.bfloat16)
    heads_here = query_weight.shape[1] // HEAD_DIM
    group_size = HEADS // KV_HEADS
    group_devices = group_size // heads_here
    head_block = keyval
    for bit_number in range(group_devices.bit_length() - 1):
        partner = partner_2(head_block, "tensor", bit_number)
        is_lower = tensor_index // (1 << bit_number) % 2 == 0
        head_block = jnp.where(
            is_lower,
            jnp.concatenate([head_block, partner], axis=0),
            jnp.concatenate([partner, head_block], axis=0),
        )
    keys_cols = head_block[:HEAD_DIM]
    values_cols = head_block[HEAD_DIM:]
    query_heads = query.reshape(row_count, heads_here, HEAD_DIM)
    scores = jnp.einsum(
        "rhd,ds->hrs", query_heads, keys_cols, preferred_element_type=jnp.float32
    ) * HEAD_DIM ** (-0.5)
    positions = jnp.arange(row_count, dtype=jnp.int32)
    allowed = (seg_ids[:, None] == seg_ids[None, :]) & (positions[None, :] <= positions[:, None])
    scores = jnp.where(allowed[None, :, :], scores, masked_score)
    weights = jax.nn.softmax(scores, axis=-1).astype(jnp.bfloat16)
    context = jnp.einsum("hrs,ds->rhd", weights, values_cols, preferred_element_type=jnp.float32)
    context = context.astype(jnp.bfloat16).reshape(row_count, col_count)
    return (wide_inputs + context.astype(jnp.float32)).astype(jnp.bfloat16)


def pick_rows(running, host_rows, source):
    flat_rows = host_rows.reshape(-1, host_rows.shape[2])
    inside = (source >= 0) & (source < flat_rows.shape[0])
    taken = jnp.take(flat_rows, jnp.clip(source, 0, flat_rows.shape[0] - 1), axis=0)
    return jnp.where(inside[:, None], taken, running)


def per_device(activations, gain, w_query, w_kv, segments, pool, row_ids, row_lengths):
    section_index = lax.axis_index("section")
    tensor_index = lax.axis_index("tensor")
    token_count = activations.shape[1]
    col_count = activations.shape[2]
    own_segments = lax.dynamic_index_in_dim(segments, section_index, 0, keepdims=False)
    after_first = attend(activations[0], gain[0], w_query[0], w_kv[0], own_segments, tensor_index)[
        None
    ]
    ends = jnp.cumsum(row_lengths)
    positions = jnp.arange(token_count, dtype=jnp.int32)
    slot = jnp.sum((positions[:, None] >= ends[None, :]).astype(jnp.int32), axis=1)
    slot_match = slot[:, None] == jnp.arange(row_ids.shape[0], dtype=jnp.int32)[None, :]
    slot_start = jnp.sum(jnp.where(slot_match, (ends - row_lengths)[None, :], 0), axis=1)
    slot_row = jnp.sum(jnp.where(slot_match, row_ids[None, :], 0), axis=1)
    source = slot_row * pool.shape[1] + positions - slot_start
    empty_rows = jnp.zeros((token_count, col_count), jnp.bfloat16)
    fresh = pick_rows(empty_rows, lax.all_gather(pool, "section", axis=0, tiled=True), source)
    handed = from_behind(after_first, "section", 1)
    second_inputs = jnp.where(section_index == 0, fresh[None], handed)
    prior_segments = lax.dynamic_index_in_dim(
        segments, jnp.maximum(section_index - 1, 0), 0, keepdims=False
    )
    second_segments = jnp.where(section_index == 0, slot, prior_segments)
    after_second = attend(
        second_inputs[0], gain[0], w_query[0], w_kv[0], second_segments, tensor_index
    )[None]
    return (after_first, after_second)


def solution(mesh):
    return jax.shard_map(
        per_device,
        mesh=mesh,
        in_specs=(
            P("section", None, "tensor"),
            P("section", "tensor"),
            P("section", None, "tensor"),
            P("section", "tensor", None),
            P(),
            P("section", None, "tensor"),
            P(),
            P(),
        ),
        out_specs=(P("section", None, "tensor"), P("section", None, "tensor")),
        check_vma=False,
    )
```

profile of v0, /device:TPU:2, one launch (start us, length us, event | category | flops | bytes accessed | tf_op | source)
XLA Modules:
  0.0 339.0 jit_solution(10043609363938623515)
XLA Ops:
  7.2 0.0 all-gather.4.cloned.1.call-start
  7.2 0.8 mul.92
  8.0 1.1 fusion.30
  9.1 34.8 %psum.14 = f32[512]{0:T(512)S(1)} all-reduce(f32[512]{0:T(512)S(1)} %fusion.30), channel_id=1, replica_groups=mesh['section'=32,'tensor'=16] {'tensor'}, use_global_device_ids=true, to_apply=%region_1.2 | all-reduce | flops 512 | bytes 4096 | tf_op jit(solution)/shard_map/psum | solution.py:33
  43.9 1.8 fusion.32
  45.7 0.0 all-gather.4.cloned.1.call-update
  45.7 0.0 all-gather.6.cloned.1.call-start
  45.8 0.7 all-gather.6.cloned.1.call-update
  46.5 0.0 all-gather.8.cloned.1.call-start
  46.6 0.7 copy.41
  47.3 0.1 reduce-window.8
  47.3 0.1 reduce
  47.5 0.7 sub.49
  48.1 0.1 convert_reduce_fusion
  48.2 0.7 select_reduce_fusion.1
  49.0 0.8 broadcast_select_fusion
  49.8 0.2 fusion.23
  50.0 73.7 %all-gather.4.cloned.1.call-done = bf16[512,4096]{1,0:T(8,128)(2,1)} async-done(((bf16[512,256]{1,0:T(8,128)(2,1)}), bf16[512,4096]{1,0:T(8,128)(2,1)}) %all-gather.4.cloned.1.call-update) | async-done | bytes 4194320 | tf_op jit(solution)/shard_map/all_gather | solution.py:38
  123.7 3.7 %fusion.16 = bf16[64,512]{1,0:T(8,128)(2,1)S(1)} fusion(bf16[512,4096]{1,0:T(8,128)(2,1)} %all-gather.4.cloned.1.call-done, bf16[1,64,4096]{2,1,0:T(8,128)(2,1)} %param.11), kind=kOutput, calls=%fused_computation.23 | convolution fusion | flops 268468224 | bytes 4784128 | tf_op jit(solution)/shard_map/dot_general | solution.py:40
  127.4 2.2 collective-permute-start
  129.6 3.9 %collective-permute-done = bf16[64,512]{1,0:T(8,128)(2,1)S(1)} collective-permute-done((bf16[64,512]{1,0:T(8,128)(2,1)S(1)}, bf16[64,512]{1,0:T(8,128)(2,1)S(1)}, u32[]{:S(2)}, u32[]{:S(2)}) %collective-permute-start) | collective-permute-done | bytes 65568 | tf_op jit(solution)/shard_map/ppermute | solution.py:21
  133.6 3.4 %collective-permute-start.1 = (bf16[128,512]{1,0:T(8,128)(2,1)S(1)}, bf16[128,512]{1,0:T(8,128)(2,1)S(1)}, u32[]{:S(2)}, u32[]{:S(2)}) collective-permute-start(bf16[128,512]{1,0:T(8,128)(2,1)S(1)} %maximum_select_fusion.2), channel_id=1, source_target_pairs={{0,2},{2,0},{1,3},{3,1},{4,6},{6,4},{5,7},{7,5},{8,10},{10,8},{9,1... | collective-permute-start | bytes 393224 | tf_op jit(solution)/shard_map/ppermute | solution.py:21
  137.0 3.5 %fusion.8 = bf16[512,256]{0,1:T(8,128)(2,1)S(1)} fusion(bf16[512,4096]{1,0:T(8,128)(2,1)} %all-gather.4.cloned.1.call-done, bf16[1,4096,256]{2,1,0:T(8,128)(2,1)S(1)} %copy-done), kind=kOutput, calls=%fused_computation.15 | convolution fusion | flops 1073872896 | bytes 6553600 | tf_op jit(solution)/shard_map/dot_general | solution.py:39
  140.5 1.4 collective-permute-done.1
  142.0 0.1 maximum_select_fusion
  142.0 0.9 fusion.63
  143.0 2.2 fusion.14
  145.2 0.2 copy.40
  145.4 0.8 fusion.33
  146.1 1.4 collective-permute-start.2
  147.6 52.3 %all-gather.6.cloned.1.call-done = bf16[64,128,256]{2,1,0:T(8,128)(2,1)} async-done(((bf16[2,128,256]{2,1,0:T(8,128)(2,1)}), bf16[64,128,256]{2,1,0:T(8,128)(2,1)}) %all-gather.6.cloned.1.call-update) | async-done | bytes 4194320 | tf_op jit(solution)/shard_map/all_gather | solution.py:96
  199.9 4.3 %gather_fusion = bf16[512,256]{1,0:T(8,128)(2,1)S(1)} fusion(bf16[8192,256]{1,0:T(8,128)(2,1)} %bitcast.129, s32[1024]{0:T(1024)S(1)} %pad_clamp_fusion), kind=kCustom, calls=%fused_computation | custom fusion | bytes 526336 | tf_op jit(solution)/shard_map/jit(_take)/gather | solution.py:75
  204.2 0.3 fusion.34
  204.5 34.3 %psum.15 = f32[512]{0:T(512)S(1)} all-reduce(f32[512]{0:T(512)S(1)} %get-tuple-element.4), channel_id=1, replica_groups=mesh['section'=32,'tensor'=16] {'tensor'}, use_global_device_ids=true, to_apply=%region_9.10 | all-reduce | flops 512 | bytes 4096 | tf_op jit(solution)/shard_map/psum | solution.py:33
  238.8 0.8 fusion.36
  239.7 70.4 %all-gather.8.cloned.1.call-done = bf16[512,4096]{1,0:T(8,128)(2,1)} async-done(((bf16[512,256]{1,0:T(8,128)(2,1)}), bf16[512,4096]{1,0:T(8,128)(2,1)}) %all-gather.8.cloned.1.call-update) | async-done | bytes 4194320 | tf_op jit(solution)/shard_map/all_gather | solution.py:38
  310.1 3.7 %fusion.17 = bf16[64,512]{1,0:T(8,128)(2,1)S(1)} fusion(bf16[512,4096]{1,0:T(8,128)(2,1)} %all-gather.8.cloned.1.call-done, bf16[1,64,4096]{2,1,0:T(8,128)(2,1)S(1)} %copy-done.3), kind=kOutput, calls=%fused_computation.24 | convolution fusion | flops 268468224 | bytes 4784128 | tf_op jit(solution)/shard_map/dot_general | solution.py:40
  313.8 2.2 collective-permute-start.3
  316.0 0.2 fusion.22
  316.2 3.8 %collective-permute-done.3 = bf16[64,512]{1,0:T(8,128)(2,1)S(1)} collective-permute-done((bf16[64,512]{1,0:T(8,128)(2,1)S(1)}, bf16[64,512]{1,0:T(8,128)(2,1)S(1)}, u32[]{:S(2)}, u32[]{:S(2)}) %collective-permute-start.3) | collective-permute-done | bytes 65568 | tf_op jit(solution)/shard_map/ppermute | solution.py:21
  320.0 3.6 %collective-permute-start.4 = (bf16[128,512]{1,0:T(8,128)(2,1)S(1)}, bf16[128,512]{1,0:T(8,128)(2,1)S(1)}, u32[]{:S(2)}, u32[]{:S(2)}) collective-permute-start(bf16[128,512]{1,0:T(8,128)(2,1)S(1)} %maximum_select_fusion.3), channel_id=1, source_target_pairs={{0,2},{2,0},{1,3},{3,1},{4,6},{6,4},{5,7},{7,5},{8,10},{10,8},{9,1... | collective-permute-start | bytes 393224 | tf_op jit(solution)/shard_map/ppermute | solution.py:21
  323.6 1.3 fusion.11
  324.9 3.4 %collective-permute-done.4 = bf16[128,512]{1,0:T(8,128)(2,1)S(1)} collective-permute-done((bf16[128,512]{1,0:T(8,128)(2,1)S(1)}, bf16[128,512]{1,0:T(8,128)(2,1)S(1)}, u32[]{:S(2)}, u32[]{:S(2)}) %collective-permute-start.4) | collective-permute-done | bytes 131104 | tf_op jit(solution)/shard_map/ppermute | solution.py:21
  328.4 0.1 maximum_select_fusion.1
  328.5 0.9 fusion.64
  329.4 2.1 fusion.15
  331.5 0.2 copy.45
  331.7 0.8 fusion.37
  (23 shorter events, 0.2 us)
Async XLA Ops:
  7.2 129.8 %copy-start = (bf16[1,4096,256]{2,1,0:T(8,128)(2,1)S(1)}, bf16[1,4096,256]{2,1,0:T(8,128)(2,1)}, u32[]{:S(2)}) copy-start(bf16[1,4096,256]{2,1,0:T(8,128)(2,1)} %param.10) | copy-start | bytes 6291460
  7.2 116.5 %all-gather.4.cloned.1.call-start = ((), (), s32[]{:S(2)}) async-start(), calls=%async_computation | async-start | bytes 4456448 | tf_op jit(solution)/shard_map/all_gather | solution.py:38
  45.7 154.1 %all-gather.6.cloned.1.call-start = ((), (), s32[]{:S(2)}) async-start(), calls=%async_computation.1 | async-start | bytes 4325376 | tf_op jit(solution)/shard_map/all_gather | solution.py:96
  46.5 263.6 %all-gather.8.cloned.1.call-start = ((), (), s32[]{:S(2)}) async-start(), calls=%async_computation.2 | async-start | bytes 4456448 | tf_op jit(solution)/shard_map/all_gather | solution.py:38
  127.4 6.2 %collective-permute-start = (bf16[64,512]{1,0:T(8,128)(2,1)S(1)}, bf16[64,512]{1,0:T(8,128)(2,1)S(1)}, u32[]{:S(2)}, u32[]{:S(2)}) collective-permute-start(bf16[64,512]{1,0:T(8,128)(2,1)S(1)} %fusion.16), channel_id=1, source_target_pairs={{0,1},{1,0},{2,3},{3,2},{4,5},{5,4},{6,7},{7,6},{8,9},{9,8},{10,11... | collective-permute-start | bytes 196616 | tf_op jit(solution)/shard_map/ppermute | solution.py:21
  133.6 8.4 %collective-permute-start.1 = (bf16[128,512]{1,0:T(8,128)(2,1)S(1)}, bf16[128,512]{1,0:T(8,128)(2,1)S(1)}, u32[]{:S(2)}, u32[]{:S(2)}) collective-permute-start(bf16[128,512]{1,0:T(8,128)(2,1)S(1)} %maximum_select_fusion.2), channel_id=1, source_target_pairs={{0,2},{2,0},{1,3},{3,1},{4,6},{6,4},{5,7},{7,5},{8,10},{10,8},{9,1... | collective-permute-start | bytes 393224 | tf_op jit(solution)/shard_map/ppermute | solution.py:21
  140.5 1.5 copy-start.5
  143.0 2.4 copy-start.2
  146.1 163.9 %copy-start.3 = (bf16[1,64,4096]{2,1,0:T(8,128)(2,1)S(1)}, bf16[1,64,4096]{2,1,0:T(8,128)(2,1)}, u32[]{:S(2)}) copy-start(bf16[1,64,4096]{2,1,0:T(8,128)(2,1)} %param.11) | copy-start | bytes 1572868
  146.1 58.0 %collective-permute-start.2 = (bf16[1,512,256]{2,1,0:T(8,128)(2,1)}, bf16[1,512,256]{2,1,0:T(8,128)(2,1)S(1)}, u32[]{:S(2)}, u32[]{:S(2)}) collective-permute-start(bf16[1,512,256]{2,1,0:T(8,128)(2,1)} %fusion.33), channel_id=1, source_target_pairs={{0,16},{16,32},{32,48},{48,64},{64,80},{80,96},{96,112},{112,128},... | collective-permute-start | bytes 786440 | tf_op jit(solution)/shard_map/ppermute | solution.py:27
  310.1 13.5 %copy-start.1 = (bf16[512,4096]{1,0:T(8,128)(2,1)S(1)}, bf16[512,4096]{1,0:T(8,128)(2,1)}, u32[]{:S(2)}) copy-start(bf16[512,4096]{1,0:T(8,128)(2,1)} %all-gather.8.cloned.1.call-done) | copy-start | bytes 12582916
  313.8 6.2 %collective-permute-start.3 = (bf16[64,512]{1,0:T(8,128)(2,1)S(1)}, bf16[64,512]{1,0:T(8,128)(2,1)S(1)}, u32[]{:S(2)}, u32[]{:S(2)}) collective-permute-start(bf16[64,512]{1,0:T(8,128)(2,1)S(1)} %fusion.17), channel_id=1, source_target_pairs={{0,1},{1,0},{2,3},{3,2},{4,5},{5,4},{6,7},{7,6},{8,9},{9,8},{10,11... | collective-permute-start | bytes 196616 | tf_op jit(solution)/shard_map/ppermute | solution.py:21
  320.0 8.4 %collective-permute-start.4 = (bf16[128,512]{1,0:T(8,128)(2,1)S(1)}, bf16[128,512]{1,0:T(8,128)(2,1)S(1)}, u32[]{:S(2)}, u32[]{:S(2)}) collective-permute-start(bf16[128,512]{1,0:T(8,128)(2,1)S(1)} %maximum_select_fusion.3), channel_id=1, source_target_pairs={{0,2},{2,0},{1,3},{3,1},{4,6},{6,4},{5,7},{7,5},{8,10},{10,8},{9,1... | collective-permute-start | bytes 393224 | tf_op jit(solution)/shard_map/ppermute | solution.py:21
  324.9 3.5 %copy-start.4 = (bf16[512,256]{0,1:T(8,128)(2,1)}, bf16[512,256]{0,1:T(8,128)(2,1)S(1)}, u32[]{:S(2)}) copy-start(bf16[512,256]{0,1:T(8,128)(2,1)S(1)} %fusion.11) | copy-start | bytes 786436
Sparse Core Ops, SparseCore 0:
  45.9 77.8 all-gather.3
  125.8 73.9 all-gather.5
  239.8 70.2 all-gather.7
where the time goes:
time: 340 us; the launch traced here: 339 us
  waiting for transfers between devices  210 us (62%)
  blocking collectives  69.1 us (20%)
  matrix products  18.4 us (5%)
  between operations  14 us (4%)
  starting transfers between devices  12.9 us (4%)
  other arithmetic  9.48 us (3%)
  local copies, waits for them, and re-layouts  5.46 us (2%)
    all_gather x2, waiting for transfers between devices, attend(): part_cols = lax.all_gather(normed, 'tensor', axis=1, tiled=True)  144 us
    psum x2, blocking collectives, attend(): lax.psum(jnp.sum(wide_inputs * wide_inputs, axis=1), 'tensor')  69.1 us
    all_gather x1, waiting for transfers between devices, per_device(): lax.all_gather(pool, 'section', axis=0, tiled=True)  52.3 us
    ppermute x4, waiting for transfers between devices, partner_2(): return lax.ppermute(block, axis, route)  12.6 us
    ppermute x4, starting transfers between devices, partner_2(): return lax.ppermute(block, axis, route)  11.3 us
    dot_general x2, matrix products, attend(): lax.dot_general(keyval_weight, part_cols, (((1,), (1,)), ((), ())), prefe...  7.42 us
  transfers between devices with their start and end apart: 8, of which 7 were waited for; matrix products, arithmetic and copies ran while one was open for 6% of the time, Pallas kernels for 0%

commit v1 on v0

--- a/solution.py
+++ b/solution.py
@@ -30,7 +30,9 @@
 def attend(inputs, gain_cols, query_weight, keyval_weight, seg_ids, tensor_index):
     row_count, col_count = inputs.shape
     wide_inputs = inputs.astype(jnp.float32)
-    square_total = lax.psum(jnp.sum(wide_inputs * wide_inputs, axis=1), "tensor")
+    square_total = jnp.sum(
+        lax.all_gather(jnp.sum(wide_inputs * wide_inputs, axis=1), "tensor"), axis=0
+    )
     row_scale = lax.rsqrt(square_total / D + norm_eps)
     normed = (wide_inputs * row_scale[:, None] * gain_cols.astype(jnp.float32)[None, :]).astype(
         jnp.bfloat16

time: 340 us -> 311 us (0.915)
  blocking collectives: 69.1 us -> 49.2 us
  waiting for transfers between devices: 210 us -> 201 us
    psum x2 -> x0, blocking collectives: 69.1 us -> none  [attend(): lax.psum(jnp.sum(wide_inputs * wide_inputs, axis=1), 'tensor')]
    all_gather x0 -> x2, blocking collectives: none -> 49.2 us  [attend(): lax.all_gather(jnp.sum(wide_inputs * wide_inputs, axis=1), 'tensor')]
    all_gather x2, waiting for transfers between devices: 144 us -> 136 us  [attend(): part_cols = lax.all_gather(normed, 'tensor', axis=1, tiled=True)]
  transfers between devices with their start and end apart: 8 -> 8, of which waited for: 7 -> 7; matrix products, arithmetic and copies ran while one was open for 6% -> 7% of each run, Pallas kernels for 0% -> 0%
where the time goes in v1:
time: 311 us
  waiting for transfers between devices  201 us (65%)
  blocking collectives  49.2 us (16%)
  matrix products  18.4 us (6%)
  between operations  14 us (5%)
  starting transfers between devices  12.9 us (4%)
  other arithmetic  9.56 us (3%)
  local copies, waits for them, and re-layouts  5.46 us (2%)
    all_gather x2, waiting for transfers between devices, attend(): part_cols = lax.all_gather(normed, 'tensor', axis=1, tiled=True)  136 us
    all_gather x1, waiting for transfers between devices, per_device(): lax.all_gather(pool, 'section', axis=0, tiled=True)  52.2 us
    all_gather x2, blocking collectives, attend(): lax.all_gather(jnp.sum(wide_inputs * wide_inputs, axis=1), 'tensor')  49.2 us
    ppermute x4, waiting for transfers between devices, partner_2(): return lax.ppermute(block, axis, route)  12.6 us
    ppermute x4, starting transfers between devices, partner_2(): return lax.ppermute(block, axis, route)  11.3 us
    dot_general x2, matrix products, attend(): lax.dot_general(keyval_weight, part_cols, (((1,), (1,)), ((), ())), prefe...  7.42 us
  transfers between devices with their start and end apart: 8, of which 7 were waited for; matrix products, arithmetic and copies ran while one was open for 7% of the time, Pallas kernels for 0%

profile of v1, /device:TPU:2, one launch (start us, length us, event | category | flops | bytes accessed | tf_op | source)
XLA Modules:
  0.0 310.9 jit_solution(14790415354478956893)
XLA Ops:
  7.2 0.0 all-gather.8.cloned.1.call-start
  7.2 0.8 mul.92
  8.0 1.1 fusion.30
  9.1 26.1 %all-gather.2 = f32[16,1,512]{2,1,0:T(1,128)S(1)} all-gather(f32[1,1,512]{2,1,0:T(1,128)S(1)} %bitcast.141), channel_id=2, replica_groups=mesh['section'=32,'tensor'=16] {'tensor'}, dimensions={0}, use_global_device_ids=true | all-gather | bytes 34816 | tf_op jit(solution)/shard_map/all_gather | solution.py:34
  35.3 1.8 fusion.32
  37.2 0.0 all-gather.10.cloned.1.call-start
  37.2 0.7 all-gather.10.cloned.1.call-update
  37.9 0.0 all-gather.12.cloned.1.call-start
  38.0 0.7 copy.41
  38.7 0.1 reduce-window.8
  38.8 0.1 reduce.2
  38.9 0.7 sub.49
  39.5 0.1 convert_reduce_fusion
  39.6 0.7 select_reduce_fusion.1
  40.4 0.8 broadcast_select_fusion
  41.2 0.2 fusion.23
  41.4 68.3 %all-gather.8.cloned.1.call-done = bf16[512,4096]{1,0:T(8,128)(2,1)} async-done(((bf16[512,256]{1,0:T(8,128)(2,1)}), bf16[512,4096]{1,0:T(8,128)(2,1)}) %all-gather.8.cloned.1.call-update) | async-done | bytes 4194320 | tf_op jit(solution)/shard_map/all_gather | solution.py:40
  109.7 3.7 %fusion.16 = bf16[64,512]{1,0:T(8,128)(2,1)S(1)} fusion(bf16[512,4096]{1,0:T(8,128)(2,1)} %all-gather.8.cloned.1.call-done, bf16[1,64,4096]{2,1,0:T(8,128)(2,1)} %param.11), kind=kOutput, calls=%fused_computation.23 | convolution fusion | flops 268468224 | bytes 4784128 | tf_op jit(solution)/shard_map/dot_general | solution.py:42
  113.4 2.2 collective-permute-start
  115.6 3.9 %collective-permute-done = bf16[64,512]{1,0:T(8,128)(2,1)S(1)} collective-permute-done((bf16[64,512]{1,0:T(8,128)(2,1)S(1)}, bf16[64,512]{1,0:T(8,128)(2,1)S(1)}, u32[]{:S(2)}, u32[]{:S(2)}) %collective-permute-start) | collective-permute-done | bytes 65568 | tf_op jit(solution)/shard_map/ppermute | solution.py:21
  119.6 3.4 %collective-permute-start.1 = (bf16[128,512]{1,0:T(8,128)(2,1)S(1)}, bf16[128,512]{1,0:T(8,128)(2,1)S(1)}, u32[]{:S(2)}, u32[]{:S(2)}) collective-permute-start(bf16[128,512]{1,0:T(8,128)(2,1)S(1)} %maximum_select_fusion.2), channel_id=1, source_target_pairs={{0,2},{2,0},{1,3},{3,1},{4,6},{6,4},{5,7},{7,5},{8,10},{10,8},{9,1... | collective-permute-start | bytes 393224 | tf_op jit(solution)/shard_map/ppermute | solution.py:21
  123.0 3.5 %fusion.8 = bf16[512,256]{0,1:T(8,128)(2,1)S(1)} fusion(bf16[512,4096]{1,0:T(8,128)(2,1)} %all-gather.8.cloned.1.call-done, bf16[1,4096,256]{2,1,0:T(8,128)(2,1)S(1)} %copy-done), kind=kOutput, calls=%fused_computation.15 | convolution fusion | flops 1073872896 | bytes 6553600 | tf_op jit(solution)/shard_map/dot_general | solution.py:41
  126.5 1.4 collective-permute-done.1
  128.0 0.1 maximum_select_fusion
  128.0 0.9 fusion.63
  129.0 2.2 fusion.14
  131.2 0.2 copy.40
  131.4 0.8 fusion.33
  132.1 1.4 collective-permute-start.2
  133.6 52.2 %all-gather.10.cloned.1.call-done = bf16[64,128,256]{2,1,0:T(8,128)(2,1)} async-done(((bf16[2,128,256]{2,1,0:T(8,128)(2,1)}), bf16[64,128,256]{2,1,0:T(8,128)(2,1)}) %all-gather.10.cloned.1.call-update) | async-done | bytes 4194320 | tf_op jit(solution)/shard_map/all_gather | solution.py:98
  185.9 4.3 %gather_fusion = bf16[512,256]{1,0:T(8,128)(2,1)S(1)} fusion(bf16[8192,256]{1,0:T(8,128)(2,1)} %bitcast.131, s32[1024]{0:T(1024)S(1)} %pad_clamp_fusion), kind=kCustom, calls=%fused_computation | custom fusion | bytes 526336 | tf_op jit(solution)/shard_map/jit(_take)/gather | solution.py:77
  190.2 0.3 fusion.34
  190.5 23.0 %all-gather.3 = f32[16,1,512]{2,1,0:T(1,128)S(1)} all-gather(f32[1,1,512]{2,1,0:T(1,128)S(1)} %bitcast.140), channel_id=3, replica_groups=mesh['section'=32,'tensor'=16] {'tensor'}, dimensions={0}, use_global_device_ids=true | all-gather | bytes 34816 | tf_op jit(solution)/shard_map/all_gather | solution.py:34
  213.5 0.8 fusion.36
  214.4 0.0 all-gather.12.cloned.1.call-update
  214.4 67.5 %all-gather.12.cloned.1.call-done = bf16[512,4096]{1,0:T(8,128)(2,1)} async-done(((bf16[512,256]{1,0:T(8,128)(2,1)}), bf16[512,4096]{1,0:T(8,128)(2,1)}) %all-gather.12.cloned.1.call-update) | async-done | bytes 4194320 | tf_op jit(solution)/shard_map/all_gather | solution.py:40
  281.9 3.7 %fusion.17 = bf16[64,512]{1,0:T(8,128)(2,1)S(1)} fusion(bf16[512,4096]{1,0:T(8,128)(2,1)} %all-gather.12.cloned.1.call-done, bf16[1,64,4096]{2,1,0:T(8,128)(2,1)S(1)} %copy-done.3), kind=kOutput, calls=%fused_computation.24 | convolution fusion | flops 268468224 | bytes 4784128 | tf_op jit(solution)/shard_map/dot_general | solution.py:42
  285.6 2.2 collective-permute-start.3
  287.8 0.2 fusion.22
  288.0 3.8 %collective-permute-done.3 = bf16[64,512]{1,0:T(8,128)(2,1)S(1)} collective-permute-done((bf16[64,512]{1,0:T(8,128)(2,1)S(1)}, bf16[64,512]{1,0:T(8,128)(2,1)S(1)}, u32[]{:S(2)}, u32[]{:S(2)}) %collective-permute-start.3) | collective-permute-done | bytes 65568 | tf_op jit(solution)/shard_map/ppermute | solution.py:21
  291.8 3.6 %collective-permute-start.4 = (bf16[128,512]{1,0:T(8,128)(2,1)S(1)}, bf16[128,512]{1,0:T(8,128)(2,1)S(1)}, u32[]{:S(2)}, u32[]{:S(2)}) collective-permute-start(bf16[128,512]{1,0:T(8,128)(2,1)S(1)} %maximum_select_fusion.3), channel_id=1, source_target_pairs={{0,2},{2,0},{1,3},{3,1},{4,6},{6,4},{5,7},{7,5},{8,10},{10,8},{9,1... | collective-permute-start | bytes 393224 | tf_op jit(solution)/shard_map/ppermute | solution.py:21
  295.4 1.3 fusion.11
  296.8 3.4 %collective-permute-done.4 = bf16[128,512]{1,0:T(8,128)(2,1)S(1)} collective-permute-done((bf16[128,512]{1,0:T(8,128)(2,1)S(1)}, bf16[128,512]{1,0:T(8,128)(2,1)S(1)}, u32[]{:S(2)}, u32[]{:S(2)}) %collective-permute-start.4) | collective-permute-done | bytes 131104 | tf_op jit(solution)/shard_map/ppermute | solution.py:21
  300.2 0.1 maximum_select_fusion.1
  300.3 0.9 fusion.64
  301.2 2.1 fusion.15
  303.4 0.2 copy.45
  303.6 0.8 fusion.37
  (25 shorter events, 0.2 us)
Async XLA Ops:
  7.2 115.8 %copy-start = (bf16[1,4096,256]{2,1,0:T(8,128)(2,1)S(1)}, bf16[1,4096,256]{2,1,0:T(8,128)(2,1)}, u32[]{:S(2)}) copy-start(bf16[1,4096,256]{2,1,0:T(8,128)(2,1)} %param.10) | copy-start | bytes 6291460
  7.2 102.5 %all-gather.8.cloned.1.call-start = ((), (), s32[]{:S(2)}) async-start(), calls=%async_computation | async-start | bytes 4456448 | tf_op jit(solution)/shard_map/all_gather | solution.py:40
  37.2 148.7 %all-gather.10.cloned.1.call-start = ((), (), s32[]{:S(2)}) async-start(), calls=%async_computation.1 | async-start | bytes 4325376 | tf_op jit(solution)/shard_map/all_gather | solution.py:98
  37.9 244.0 %all-gather.12.cloned.1.call-start = ((), (), s32[]{:S(2)}) async-start(), calls=%async_computation.2 | async-start | bytes 4456448 | tf_op jit(solution)/shard_map/all_gather | solution.py:40
  113.4 6.2 %collective-permute-start = (bf16[64,512]{1,0:T(8,128)(2,1)S(1)}, bf16[64,512]{1,0:T(8,128)(2,1)S(1)}, u32[]{:S(2)}, u32[]{:S(2)}) collective-permute-start(bf16[64,512]{1,0:T(8,128)(2,1)S(1)} %fusion.16), channel_id=1, source_target_pairs={{0,1},{1,0},{2,3},{3,2},{4,5},{5,4},{6,7},{7,6},{8,9},{9,8},{10,11... | collective-permute-start | bytes 196616 | tf_op jit(solution)/shard_map/ppermute | solution.py:21
  119.6 8.4 %collective-permute-start.1 = (bf16[128,512]{1,0:T(8,128)(2,1)S(1)}, bf16[128,512]{1,0:T(8,128)(2,1)S(1)}, u32[]{:S(2)}, u32[]{:S(2)}) collective-permute-start(bf16[128,512]{1,0:T(8,128)(2,1)S(1)} %maximum_select_fusion.2), channel_id=1, source_target_pairs={{0,2},{2,0},{1,3},{3,1},{4,6},{6,4},{5,7},{7,5},{8,10},{10,8},{9,1... | collective-permute-start | bytes 393224 | tf_op jit(solution)/shard_map/ppermute | solution.py:21
  126.5 1.5 copy-start.5
  129.0 2.4 copy-start.2
  132.1 149.8 %copy-start.3 = (bf16[1,64,4096]{2,1,0:T(8,128)(2,1)S(1)}, bf16[1,64,4096]{2,1,0:T(8,128)(2,1)}, u32[]{:S(2)}) copy-start(bf16[1,64,4096]{2,1,0:T(8,128)(2,1)} %param.11) | copy-start | bytes 1572868
  132.1 58.0 %collective-permute-start.2 = (bf16[1,512,256]{2,1,0:T(8,128)(2,1)}, bf16[1,512,256]{2,1,0:T(8,128)(2,1)S(1)}, u32[]{:S(2)}, u32[]{:S(2)}) collective-permute-start(bf16[1,512,256]{2,1,0:T(8,128)(2,1)} %fusion.33), channel_id=1, source_target_pairs={{0,16},{16,32},{32,48},{48,64},{64,80},{80,96},{96,112},{112,128},... | collective-permute-start | bytes 786440 | tf_op jit(solution)/shard_map/ppermute | solution.py:27
  281.9 13.5 %copy-start.1 = (bf16[512,4096]{1,0:T(8,128)(2,1)S(1)}, bf16[512,4096]{1,0:T(8,128)(2,1)}, u32[]{:S(2)}) copy-start(bf16[512,4096]{1,0:T(8,128)(2,1)} %all-gather.12.cloned.1.call-done) | copy-start | bytes 12582916
  285.6 6.2 %collective-permute-start.3 = (bf16[64,512]{1,0:T(8,128)(2,1)S(1)}, bf16[64,512]{1,0:T(8,128)(2,1)S(1)}, u32[]{:S(2)}, u32[]{:S(2)}) collective-permute-start(bf16[64,512]{1,0:T(8,128)(2,1)S(1)} %fusion.17), channel_id=1, source_target_pairs={{0,1},{1,0},{2,3},{3,2},{4,5},{5,4},{6,7},{7,6},{8,9},{9,8},{10,11... | collective-permute-start | bytes 196616 | tf_op jit(solution)/shard_map/ppermute | solution.py:21
  291.8 8.4 %collective-permute-start.4 = (bf16[128,512]{1,0:T(8,128)(2,1)S(1)}, bf16[128,512]{1,0:T(8,128)(2,1)S(1)}, u32[]{:S(2)}, u32[]{:S(2)}) collective-permute-start(bf16[128,512]{1,0:T(8,128)(2,1)S(1)} %maximum_select_fusion.3), channel_id=1, source_target_pairs={{0,2},{2,0},{1,3},{3,1},{4,6},{6,4},{5,7},{7,5},{8,10},{10,8},{9,1... | collective-permute-start | bytes 393224 | tf_op jit(solution)/shard_map/ppermute | solution.py:21
  296.8 3.5 %copy-start.4 = (bf16[512,256]{0,1:T(8,128)(2,1)}, bf16[512,256]{0,1:T(8,128)(2,1)S(1)}, u32[]{:S(2)}) copy-start(bf16[512,256]{0,1:T(8,128)(2,1)S(1)} %fusion.11) | copy-start | bytes 786436
Sparse Core Ops, SparseCore 0:
  37.3 72.3 all-gather.7
  111.8 73.9 all-gather.9
  214.5 67.3 all-gather.11
